TPU v7x, 32 devices: a whole 2x2x4 slice. The times are simulated.
32 devices in a mesh: groups: 2 (over x), lon: 16 (over z, y, core).
Axes of the slice: x: 2, y: 2, z: 4, core: 2. Of those that a mesh axis runs over, the one named last changes fastest.
Arguments:
- fields: bfloat16 [128, 512, 256], P('groups', 'lon'), parts along dimension 0, may hold values from -36 to 36
- sea_mask: int32 [128, 512], P('groups', 'lon'), parts along dimension 0, may hold values 0 or 1
- cotangent: bfloat16 [128, 512, 256], P('groups', 'lon'), parts along dimension 0, may hold values from -6 to 6
- depth_kernel: float32 [7, 7, 256], replicated, may hold values from -0.875 to 0.875
- norm_gain: float32 [256], replicated, may hold values from 0.1 to 1.9
- up_weight: bfloat16 [256, 1024], replicated, may hold values from -0.375 to 0.375
- down_weight: bfloat16 [256, 1024], replicated, may hold values from -0.1875 to 0.1875
- layer_scale: float32 [256], replicated, may hold values from 0.3 to 3
Outputs:
- grad_fields: bfloat16 [128, 512, 256], P('groups', 'lon'), parts along dimension 0
- grad_kernel: float32 [14, 7, 256], P('groups'), parts along dimension 0
- grad_up: float32 [256, 2048], P('lon', 'groups'), parts along dimension 1
- grad_down: float32 [256, 2048], P('lon', 'groups'), parts along dimension 1
There are 2 independent parts, one for each index of `groups`. A program takes and returns all parts, laid end to end along the dimension named above; an argument that names none is the same for every part. Nothing has to cross between parts.
All inputs are finite; a program needn't handle non-finite values. No bound on the sum of `sea_mask` on one device may be relied on, other than what follows from the above.
Results may differ from a plain program's by a relative error of at most 0.0063.
Values may be sent and summed in bfloat16 or wider, within the bound.
A program may use at most 128 MiB of HBM per device.

v0:
```python
import math
import jax
import jax.numpy as jnp
from jax import lax
from jax.sharding import PartitionSpec as P


def from_partner(block, axis, bit):
    count = lax.axis_size(axis)
    route = []
    for low in range(count):
        high = low | 1 << bit
        if high != low and high < count:
            route += [(low, high), (high, low)]
    return lax.ppermute(block, axis, route)


def extended_2(cells, sides, width):
    for axis, dim in sides:
        count = lax.axis_size(axis)
        head = lax.slice_in_dim(cells, 0, width, axis=dim)
        tail = lax.slice_in_dim(cells, cells.shape[dim] - width, cells.shape[dim], axis=dim)
        cells = jnp.concatenate(
            [
                lax.ppermute(tail, axis, [(i, (i + 1) % count) for i in range(count)]),
                cells,
                lax.ppermute(head, axis, [((i + 1) % count, i) for i in range(count)]),
            ],
            axis=dim,
        )
    return cells


def gelu_tanh(values):
    return jax.nn.gelu(values, approximate=True)


def local(
    fields, sea_mask, cotangent, depth_kernel, norm_gain, up_weight, down_weight, layer_scale
):
    band_rows, band_cols, channels = fields.shape
    devices = lax.axis_size("lon")
    mask_bf = sea_mask.astype(jnp.bfloat16)[:, :, None]
    masked = fields * mask_bf
    seam_rows = masked[band_rows - 3 :]
    partner_rows = seam_rows
    for bit in range(devices.bit_length() - 1):
        partner_rows = from_partner(partner_rows, "lon", bit)
    ghost = partner_rows[::-1, ::-1]
    south = jnp.zeros((3, band_cols, channels), jnp.bfloat16)
    padded = jnp.concatenate([south, masked, ghost], axis=0)
    extended = extended_2(padded, (("lon", 1),), 3)
    ext_wide = extended.astype(jnp.float32)
    conv = jnp.zeros((band_rows, band_cols, channels), jnp.float32)
    for row_tap in range(7):
        for col_tap in range(7):
            conv = (
                conv
                + depth_kernel[row_tap, col_tap]
                * ext_wide[row_tap : row_tap + band_rows, col_tap : col_tap + band_cols]
            )
    mean_z = jnp.mean(conv, axis=-1, keepdims=True)
    centred = conv - mean_z
    inv_std = lax.rsqrt(jnp.mean(centred * centred, axis=-1, keepdims=True) + 1e-06)
    nhat = centred * inv_std
    cells = band_rows * band_cols
    normed = (nhat * norm_gain).astype(jnp.bfloat16).reshape(cells, channels)
    dout = (
        (cotangent.astype(jnp.float32) * layer_scale * mask_bf.astype(jnp.float32))
        .astype(jnp.bfloat16)
        .reshape(cells, channels)
    )
    preact = jnp.dot(normed, up_weight, preferred_element_type=jnp.float32)
    hidden = gelu_tanh(preact).astype(jnp.bfloat16)
    dhid = jnp.dot(dout, down_weight, preferred_element_type=jnp.float32)
    _, back = jax.vjp(gelu_tanh, preact)
    dpre = back(dhid)[0].astype(jnp.bfloat16)
    contract_rows = (((0,), (0,)), ((), ()))
    contract_cols = (((1,), (1,)), ((), ()))
    factor = 1.0 / math.sqrt(cells * devices)
    hidden_width = up_weight.shape[1]
    term_up = lax.dot_general(normed, dpre, contract_rows, preferred_element_type=jnp.float32)
    term_down = lax.dot_general(dout, hidden, contract_rows, preferred_element_type=jnp.float32)
    owned = lax.psum_scatter(
        jnp.concatenate([term_up, term_down], axis=1) * factor,
        "lon",
        scatter_dimension=0,
        tiled=True,
    )
    grad_up = owned[:, :hidden_width]
    grad_down = owned[:, hidden_width:]
    dnorm = lax.dot_general(dpre, up_weight, contract_cols, preferred_element_type=jnp.float32)
    scaled = dnorm.reshape(band_rows, band_cols, channels) * norm_gain
    grad_conv = inv_std * (
        scaled
        - jnp.mean(scaled, axis=-1, keepdims=True)
        - nhat * jnp.mean(scaled * nhat, axis=-1, keepdims=True)
    )
    taps = []
    for row_tap in range(7):
        for col_tap in range(7):
            taps.append(
                jnp.sum(
                    grad_conv
                    * ext_wide[row_tap : row_tap + band_rows, col_tap : col_tap + band_cols],
                    axis=(0, 1),
                )
            )
    local_kernel = jnp.stack(taps, axis=0).reshape(7, 7, channels) * factor
    grad_kernel = lax.psum(local_kernel, "lon")
    grad_pad = jnp.pad(grad_conv, ((6, 6), (6, 6), (0, 0)))
    grad_ext = jnp.zeros((band_rows + 6, band_cols + 6, channels), jnp.float32)
    for row_tap in range(7):
        for col_tap in range(7):
            grad_ext = (
                grad_ext
                + depth_kernel[row_tap, col_tap]
                * grad_pad[
                    6 - row_tap : 12 - row_tap + band_rows, 6 - col_tap : 12 - col_tap + band_cols
                ]
            )
    rims = jnp.concatenate([grad_ext[:, :3], grad_ext[:, band_cols + 3 :]], axis=1)
    arrived = extended_2(rims.astype(jnp.bfloat16), (("lon", 1),), 3).astype(rims.dtype)
    grad_padded = grad_ext[:, 3 : band_cols + 3]
    grad_padded = grad_padded.at[:, :3].add(arrived[:, :3])
    grad_padded = grad_padded.at[:, band_cols - 3 :].add(arrived[:, 9:])
    seam_grads = grad_padded[band_rows + 3 :]
    partner_grads = seam_grads
    for bit in range(devices.bit_length() - 1):
        partner_grads = from_partner(partner_grads.astype(jnp.bfloat16), "lon", bit).astype(
            partner_grads.dtype
        )
    grad_masked = grad_padded[3 : band_rows + 3]
    grad_masked = grad_masked.at[band_rows - 3 :].add(partner_grads[::-1, ::-1])
    grad_fields = (
        cotangent.astype(jnp.float32) + mask_bf.astype(jnp.float32) * grad_masked
    ).astype(jnp.bfloat16)
    return (grad_fields, grad_kernel, grad_up, grad_down)


def solution(mesh):
    return jax.shard_map(
        local,
        mesh=mesh,
        in_specs=(
            P("groups", "lon", None),
            P("groups", "lon"),
            P("groups", "lon", None),
            P(),
            P(),
            P(),
            P(),
            P(),
        ),
        out_specs=(
            P("groups", "lon", None),
            P("groups", None, None),
            P("lon", "groups"),
            P("lon", "groups"),
        ),
        check_vma=False,
    )
```

profile of v0, /device:TPU:0, one launch (start us, length us, event | category | flops | bytes accessed | tf_op | source)
XLA Modules:
  0.0 221.3 jit_solution(10699872550884711838)
XLA Ops:
  11.2 2.9 %collective-permute-start.1 = (bf16[3,32,256]{2,1,0:T(8,128)(2,1)S(1)}, bf16[3,32,256]{2,1,0:T(8,128)(2,1)S(1)}, u32[]{:S(2)}, u32[]{:S(2)}) collective-permute-start(bf16[3,32,256]{2,1,0:T(8,128)(2,1)S(1)} %collective-permute-done), channel_id=1, source_target_pairs={{0,2},{2,0},{1,3},{3,1},{4,6},{6,4},{5,7},{7,5},{8,10},{10,8},{9,1... | collective-permute-start | bytes 147464 | tf_op jit(solution)/shard_map/ppermute | solution.py:15
  16.1 2.1 collective-permute-start.2
  18.3 2.0 collective-permute-done.2
  20.3 3.0 %collective-permute-start.3 = (bf16[3,32,256]{2,1,0:T(8,128)(2,1)S(1)}, bf16[3,32,256]{2,1,0:T(8,128)(2,1)S(1)}, u32[]{:S(2)}, u32[]{:S(2)}) collective-permute-start(bf16[3,32,256]{2,1,0:T(8,128)(2,1)S(1)} %collective-permute-done.2), channel_id=1, source_target_pairs={{0,8},{8,0},{1,9},{9,1},{2,10},{10,2},{3,11},{11,3},{4,12},{12,4},... | collective-permute-start | bytes 147464 | tf_op jit(solution)/shard_map/ppermute | solution.py:15
  25.6 4.4 %collective-permute-start.5 = (bf16[70,3,256]{2,1,0:T(4,128)(2,1)S(1)}, bf16[70,3,256]{2,1,0:T(4,128)(2,1)S(1)}, u32[]{:S(2)}, u32[]{:S(2)}) collective-permute-start(bf16[70,3,256]{2,1,0:T(4,128)(2,1)S(1)} %get-tuple-element.97), channel_id=1, source_target_pairs={{1,0},{2,1},{3,2},{4,3},{5,4},{6,5},{7,6},{8,7},{9,8},{10,9},{11,1... | collective-permute-start | bytes 322568 | tf_op jit(solution)/shard_map/ppermute | solution.py:27
  30.3 2.7 %collective-permute-done.4 = bf16[70,3,256]{2,1,0:T(4,128)(2,1)S(1)} collective-permute-done((bf16[70,3,256]{2,1,0:T(4,128)(2,1)S(1)}, bf16[70,3,256]{2,1,0:T(4,128)(2,1)S(1)}, u32[]{:S(2)}, u32[]{:S(2)}) %collective-permute-start.4) | collective-permute-done | bytes 107552 | tf_op jit(solution)/shard_map/ppermute | solution.py:25
  35.2 15.9 %fusion.115 = (f32[64,32]{1,0:T(8,128)S(1)}, f32[64,32,256]{2,1,0:T(8,128)}) fusion(f32[70,38,256]{2,1,0:T(8,128)S(1)} %maximum_convert_fusion, f32[256]{0:T(256)S(1)} %bitcast.211, f32[256]{0:T(256)S(1)} %bitcast.213, f32[256]{0:T(256)S(1)} %bitcast.119, f32[256]{0:T(256)S(1)} %bitcast.121, f32[256]{0:T(256)S(1)} %bitcast.123, f32[256]{0:T(256)S(1)} %bitcast.125, ...), kind=kLoop, calls=%fused_computation.242 | loop fusion | flops 51378176 | bytes 104915968 | tf_op jit(solution)/shard_map/reduce_sum | solution.py:62
  51.1 2.4 %multiply_reduce_fusion.51 = f32[64,32]{1,0:T(8,128)S(1)} fusion(f32[64,32,256]{2,1,0:T(8,128)} %get-tuple-element.93, f32[64,32]{1,0:T(8,128)S(1)} %broadcast_multiply_fusion.3), kind=kLoop, calls=%fused_computation.216 | loop fusion | flops 1570816 | bytes 2113536 | tf_op jit(solution)/shard_map/reduce_sum | solution.py:64
  55.9 4.2 %fusion.7 = f32[256,1024]{1,0:T(8,128)} fusion(bf16[2048,256]{1,0:T(8,128)(2,1)S(1)} %bitcast.115, f32[2048,1024]{1,0:T(8,128)S(1)} %fusion.121), kind=kOutput, calls=%fused_computation.59 | convolution fusion | flops 1092616192 | bytes 10485760 | tf_op jit(solution)/shard_map/dot_general | solution.py:83
  60.1 6.3 %fusion.6 = bf16[2048,1024]{1,0:T(8,128)(2,1)S(1)} fusion(f32[2048,1024]{1,0:T(8,128)S(1)} %fusion.121, bf16[2048,256]{1,0:T(8,128)(2,1)S(1)} %bitcast.116, bf16[256,1024]{1,0:T(8,128)(2,1)S(1)} %copy-done.109), kind=kOutput, calls=%fused_computation.57 | convolution fusion | flops 1115684864 | bytes 14155776 | tf_op jit(solution)/shard_map/dot_general | solution.py:75
  66.3 2.6 %multiply_reduce_fusion.50 = (f32[2048]{0:T(1024)S(1)}, f32[2048,256]{1,0:T(8,128)}) fusion(f32[256]{0:T(256)S(1)} %copy-done.17, bf16[2048,1024]{1,0:T(8,128)(2,1)S(1)} %fusion.6, bf16[256,1024]{1,0:T(8,128)(2,1)S(1)} %copy-done), kind=kOutput, calls=%fused_computation.214 | convolution fusion | flops 1074788352 | bytes 6824960 | tf_op jit(solution)/shard_map/dot_general | solution.py:92
  69.1 2.9 %multiply_reduce_fusion.49 = f32[64,32]{1,0:T(8,128)S(1)} fusion(f32[64,32,256]{2,1,0:T(8,128)} %bitcast.112, f32[64,32,256]{2,1,0:T(8,128)} %get-tuple-element.93, f32[256]{0:T(256)S(1)} %copy-done.17, f32[64,32]{1,0:T(8,128)S(1)} %add_rsqrt_fusion, f32[64,32]{1,0:T(8,128)S(1)} %broadcast_multiply_fusion.3), kind=kLoop, calls=%fused_computation.213 | loop fusion | flops 2619392 | bytes 4219904 | tf_op jit(solution)/shard_map/reduce_sum | solution.py:97
  72.9 6.6 %multiply_reduce_fusion = (f32[256]{0:T(256)}, f32[256]{0:T(256)}, f32[256]{0:T(256)}, f32[256]{0:T(256)}, f32[256]{0:T(256)}, /*index=5*/f32[256]{0:T(256)}, f3...) fusion(f32[70,38,256]{2,1,0:T(8,128)S(1)} %maximum_convert_fusi, ...), kind=kLoop, calls=%fused_computation.163 | loop fusion | flops 22539776 | bytes 44092416 | tf_op jit(solution)/shard_map/reduce_sum | solution.py:103
  79.9 22.2 %fusion.113 = (bf16[70,38,256]{2,1,0:T(8,128)(2,1)S(1)}, f32[70,38,256]{2,1,0:T(8,128)S(1)}) fusion(f32[256]{0:T(256)S(1)} %bitcast.212, f32[256]{0:T(256)S(1)} %bitcast.214, f32[256]{0:T(256)S(1)} %bitcast.120, f32[256]{0:T(256)S(1)} %bitcast.122, f32[256]{0:T(256)S(1)} %bitcast.124, f32[256]{0:T(256)S(1)} %bitcast.126, f32[256]{0:T(256)S(1)} %bitcast.128, ...), kind=kLoop, calls=%fused_computation.241 | loop fusion | flops 66734080 | bytes 6233088 | tf_op jit(solution)/shard_map/convert.3
  103.0 3.8 %collective-permute-start.7 = (bf16[70,3,256]{2,1,0:T(4,128)(2,1)S(1)}, bf16[70,3,256]{2,1,0:T(4,128)(2,1)S(1)}, u32[]{:S(2)}, u32[]{:S(2)}) collective-permute-start(bf16[70,3,256]{2,1,0:T(4,128)(2,1)S(1)} %get-tuple-element.95), channel_id=1, source_target_pairs={{1,0},{2,1},{3,2},{4,3},{5,4},{6,5},{7,6},{8,7},{9,8},{10,9},{11,1... | collective-permute-start | bytes 322568 | tf_op jit(solution)/shard_map/ppermute | solution.py:27
  106.8 4.5 %fusion.122 = f32[256,1024]{1,0:T(8,128)} fusion(bf16[2048,256]{1,0:T(8,128)(2,1)S(1)} %bitcast.114, bf16[2048,1024]{1,0:T(8,128)(2,1)} %copy-done.110), kind=kOutput, calls=%fused_computation.249 | convolution fusion | flops 1073741824 | bytes 6291456 | tf_op jit(solution)/shard_map/dot_general | solution.py:82
  115.4 5.2 %scatter-add.10 = f32[70,32,256]{2,1,0:T(8,128)} dynamic-update-slice(f32[70,32,256]{2,1,0:T(8,128)} %slice.866, f32[70,3,256]{2,1,0:T(4,128)} %convert_add_fusion.1, s32[]{:T(128)} %constant.108.clone.1, s32[]{:T(128)} %constant.108.clone.1, s32[]{:T(128)} %constant.108.clone.1) | dynamic-update-slice | bytes 430084 | tf_op jit(solution)/shard_map/scatter-add | solution.py:125
  120.6 2.1 slice_add_fusion
  122.8 4.6 %scatter-add.11 = f32[70,32,256]{2,1,0:T(8,128)} dynamic-update-slice(f32[70,32,256]{2,1,0:T(8,128)} %scatter-add.10, f32[70,3,256]{2,1,0:T(4,128)} %slice_add_fusion, s32[]{:T(128)} %constant.108.clone.1, s32[]{:T(128)} %constant.109.clone.1, s32[]{:T(128)} %constant.108.clone.1) | dynamic-update-slice | bytes 430084 | tf_op jit(solution)/shard_map/scatter-add | solution.py:126
  128.2 3.2 %maximum_multiply_fusion = f32[256,2048]{1,0:T(8,128)} fusion(f32[256,1024]{1,0:T(8,128)} %fusion.7, f32[256,1024]{1,0:T(8,128)} %fusion.122), kind=kLoop, calls=%fused_computation.162 | loop fusion | flops 1048576 | bytes 4194304 | tf_op jit(solution)/shard_map/mul | solution.py:85
  131.5 6.1 %multiply_reduce_fusion.18 = (f32[256]{0:T(256)S(1)}, f32[256]{0:T(256)S(1)}, f32[256]{0:T(256)S(1)}, f32[256]{0:T(256)S(1)}, f32[256]{0:T(256)S(1)}, /*index=5*...) fusion(f32[64,32,256]{2,1,0:T(8,128)} %copy-done.3, ...), kind=kLoop, calls=%fused_computation.181 | loop fusion | flops 18869760 | bytes 39864320 | tf_op jit(solution)/shard_map/reduce_sum | solution.py:103
  138.0 4.3 %multiply_reduce_fusion.36 = (f32[256]{0:T(256)S(1)}, f32[256]{0:T(256)S(1)}, f32[256]{0:T(256)S(1)}, f32[256]{0:T(256)S(1)}, f32[256]{0:T(256)}, /*index=5*/f32...) fusion(f32[64,32,256]{2,1,0:T(8,128)S(1)} %copy-done.4, ...), kind=kLoop, calls=%fused_computation.199 | loop fusion | flops 13628160 | bytes 29373440 | tf_op jit(solution)/shard_map/reduce_sum | solution.py:103
  145.8 61.8 %psum.7 = f32[7,7,256]{2,1,0:T(8,128)} all-reduce(f32[7,7,256]{2,1,0:T(8,128)S(1)} %mul.1497), channel_id=1, replica_groups=mesh['groups'=2,'lon'=16] {'lon'}, use_global_device_ids=true, to_apply=%region_53.0 | all-reduce | flops 12544 | bytes 100352 | tf_op jit(solution)/shard_map/psum | solution.py:110
  210.4 2.5 %fusion.107 = bf16[64,32,256]{2,1,0:T(8,128)(2,1)} fusion(bf16[64,32,256]{2,1,0:T(8,128)(2,1)} %param.16, f32[64,32,256]{2,1,0:T(8,128)S(1)} %fusion.108, f32[64,32]{1,0:T(8,128)S(1)} %copy-done.15), kind=kLoop, calls=%fused_computation.161 | loop fusion | flops 2097152 | bytes 4202496 | tf_op jit(solution)/shard_map/convert_element_type | solution.py:137
  (273 shorter events, 27.2 us)
Async XLA Ops:
  7.2 47.1 %copy-start = (bf16[256,1024]{1,0:T(8,128)(2,1)S(1)}, bf16[256,1024]{1,0:T(8,128)(2,1)}, u32[]{:S(2)}) copy-start(bf16[256,1024]{1,0:T(8,128)(2,1)} %param.19) | copy-start | bytes 1572868
  7.2 205.7 %reduce-scatter.2.cloned.1.call-start = ((), (), s32[]{:S(2)}) async-start(), calls=%async_computation.1 | async-start | bytes 2228224 | tf_op jit(solution)/shard_map/reduce_scatter | solution.py:84
  9.8 23.2 %copy-start.5 = (bf16[64,32,256]{2,1,0:T(8,128)(2,1)}, bf16[64,32,256]{2,1,0:T(8,128)(2,1)S(1)}, u32[]{:S(2)}) copy-start(bf16[64,32,256]{2,1,0:T(8,128)(2,1)S(1)} %broadcast_multiply_fusion) | copy-start | bytes 3145732
  9.8 1.4 collective-permute-start
  10.4 22.6 %copy-start.14 = (f32[64,32]{1,0:T(8,128)}, f32[64,32]{1,0:T(8,128)S(1)}, u32[]{:S(2)}) copy-start(f32[64,32]{1,0:T(8,128)S(1)} %copy.14) | copy-start | bytes 24580
  11.2 4.9 %collective-permute-start.1 = (bf16[3,32,256]{2,1,0:T(8,128)(2,1)S(1)}, bf16[3,32,256]{2,1,0:T(8,128)(2,1)S(1)}, u32[]{:S(2)}, u32[]{:S(2)}) collective-permute-start(bf16[3,32,256]{2,1,0:T(8,128)(2,1)S(1)} %collective-permute-done), channel_id=1, source_target_pairs={{0,2},{2,0},{1,3},{3,1},{4,6},{6,4},{5,7},{7,5},{8,10},{10,8},{9,1... | collective-permute-start | bytes 147464 | tf_op jit(solution)/shard_map/ppermute | solution.py:15
  16.1 4.1 %collective-permute-start.2 = (bf16[3,32,256]{2,1,0:T(8,128)(2,1)S(1)}, bf16[3,32,256]{2,1,0:T(8,128)(2,1)S(1)}, u32[]{:S(2)}, u32[]{:S(2)}) collective-permute-start(bf16[3,32,256]{2,1,0:T(8,128)(2,1)S(1)} %collective-permute-done.1), channel_id=1, source_target_pairs={{0,4},{4,0},{1,5},{5,1},{2,6},{6,2},{3,7},{7,3},{8,12},{12,8},{9,1... | collective-permute-start | bytes 147464 | tf_op jit(solution)/shard_map/ppermute | solution.py:15
  18.2 16.6 %copy-start.18 = (f32[1,1,256]{2,1,0:T(1,128)}, f32[1,1,256]{2,1,0:T(1,128)S(1)}, u32[]{:S(2)}) copy-start(f32[1,1,256]{2,1,0:T(1,128)S(1)} %get-tuple-element.113) | copy-start | bytes 3076
  18.2 16.6 %copy-start.20 = (f32[1,1,256]{2,1,0:T(1,128)}, f32[1,1,256]{2,1,0:T(1,128)S(1)}, u32[]{:S(2)}) copy-start(f32[1,1,256]{2,1,0:T(1,128)S(1)} %get-tuple-element.114) | copy-start | bytes 3076
  18.2 16.6 %copy-start.22 = (f32[1,1,256]{2,1,0:T(1,128)}, f32[1,1,256]{2,1,0:T(1,128)S(1)}, u32[]{:S(2)}) copy-start(f32[1,1,256]{2,1,0:T(1,128)S(1)} %get-tuple-element.115) | copy-start | bytes 3076
  18.2 16.6 %copy-start.24 = (f32[1,1,256]{2,1,0:T(1,128)}, f32[1,1,256]{2,1,0:T(1,128)S(1)}, u32[]{:S(2)}) copy-start(f32[1,1,256]{2,1,0:T(1,128)S(1)} %get-tuple-element.116) | copy-start | bytes 3076
  18.2 16.6 %copy-start.26 = (f32[1,1,256]{2,1,0:T(1,128)}, f32[1,1,256]{2,1,0:T(1,128)S(1)}, u32[]{:S(2)}) copy-start(f32[1,1,256]{2,1,0:T(1,128)S(1)} %get-tuple-element.117) | copy-start | bytes 3076
  18.3 16.6 %copy-start.28 = (f32[1,1,256]{2,1,0:T(1,128)}, f32[1,1,256]{2,1,0:T(1,128)S(1)}, u32[]{:S(2)}) copy-start(f32[1,1,256]{2,1,0:T(1,128)S(1)} %get-tuple-element.118) | copy-start | bytes 3076
  20.3 5.1 %collective-permute-start.3 = (bf16[3,32,256]{2,1,0:T(8,128)(2,1)S(1)}, bf16[3,32,256]{2,1,0:T(8,128)(2,1)S(1)}, u32[]{:S(2)}, u32[]{:S(2)}) collective-permute-start(bf16[3,32,256]{2,1,0:T(8,128)(2,1)S(1)} %collective-permute-done.2), channel_id=1, source_target_pairs={{0,8},{8,0},{1,9},{9,1},{2,10},{10,2},{3,11},{11,3},{4,12},{12,4},... | collective-permute-start | bytes 147464 | tf_op jit(solution)/shard_map/ppermute | solution.py:15
  25.6 7.4 %collective-permute-start.4 = (bf16[70,3,256]{2,1,0:T(4,128)(2,1)S(1)}, bf16[70,3,256]{2,1,0:T(4,128)(2,1)S(1)}, u32[]{:S(2)}, u32[]{:S(2)}) collective-permute-start(bf16[70,3,256]{2,1,0:T(4,128)(2,1)S(1)} %get-tuple-element.96), channel_id=1, source_target_pairs={{0,1},{1,2},{2,3},{3,4},{4,5},{5,6},{6,7},{7,8},{8,9},{9,10},{10,1... | collective-permute-start | bytes 322568 | tf_op jit(solution)/shard_map/ppermute | solution.py:25
  25.6 7.3 %collective-permute-start.5 = (bf16[70,3,256]{2,1,0:T(4,128)(2,1)S(1)}, bf16[70,3,256]{2,1,0:T(4,128)(2,1)S(1)}, u32[]{:S(2)}, u32[]{:S(2)}) collective-permute-start(bf16[70,3,256]{2,1,0:T(4,128)(2,1)S(1)} %get-tuple-element.97), channel_id=1, source_target_pairs={{1,0},{2,1},{3,2},{4,3},{5,4},{6,5},{7,6},{8,7},{9,8},{10,9},{11,1... | collective-permute-start | bytes 322568 | tf_op jit(solution)/shard_map/ppermute | solution.py:27
  79.5 22.6 %copy-start.3 = (f32[64,32,256]{2,1,0:T(8,128)}, f32[64,32,256]{2,1,0:T(8,128)S(1)}, u32[]{:S(2)}) copy-start(f32[64,32,256]{2,1,0:T(8,128)S(1)} %get-tuple-element.89) | copy-start | bytes 6291460
  79.8 26.9 %copy-start.8 = (bf16[64,32,256]{2,1,0:T(8,128)(2,1)S(1)}, bf16[64,32,256]{2,1,0:T(8,128)(2,1)}, u32[]{:S(2)}) copy-start(bf16[64,32,256]{2,1,0:T(8,128)(2,1)} %copy-done.7) | copy-start | bytes 3145732
  102.3 10.8 %collective-permute-start.6 = (bf16[70,3,256]{2,1,0:T(4,128)(2,1)S(1)}, bf16[70,3,256]{2,1,0:T(4,128)(2,1)S(1)}, u32[]{:S(2)}, u32[]{:S(2)}) collective-permute-start(bf16[70,3,256]{2,1,0:T(4,128)(2,1)S(1)} %get-tuple-element.94), channel_id=1, source_target_pairs={{0,1},{1,2},{2,3},{3,4},{4,5},{5,6},{6,7},{7,8},{8,9},{9,10},{10,1... | collective-permute-start | bytes 322568 | tf_op jit(solution)/shard_map/ppermute | solution.py:25
  103.0 10.1 %collective-permute-start.7 = (bf16[70,3,256]{2,1,0:T(4,128)(2,1)S(1)}, bf16[70,3,256]{2,1,0:T(4,128)(2,1)S(1)}, u32[]{:S(2)}, u32[]{:S(2)}) collective-permute-start(bf16[70,3,256]{2,1,0:T(4,128)(2,1)S(1)} %get-tuple-element.95), channel_id=1, source_target_pairs={{1,0},{2,1},{3,2},{4,3},{5,4},{6,5},{7,6},{8,7},{9,8},{10,9},{11,1... | collective-permute-start | bytes 322568 | tf_op jit(solution)/shard_map/ppermute | solution.py:27
  128.2 3.2 %collective-permute-start.8 = (bf16[3,32,256]{2,1,0:T(8,128)(2,1)S(1)}, bf16[3,32,256]{2,1,0:T(8,128)(2,1)}, u32[]{:S(2)}, u32[]{:S(2)}) collective-permute-start(bf16[3,32,256]{2,1,0:T(8,128)(2,1)S(1)} %slice.1409), channel_id=1, source_target_pairs={{0,1},{1,0},{2,3},{3,2},{4,5},{5,4},{6,7},{7,6},{8,9},{9,8},{10,11... | collective-permute-start | bytes 147464 | tf_op jit(solution)/shard_map/ppermute | solution.py:15
  131.5 6.4 %collective-permute-start.9 = (bf16[3,32,256]{2,1,0:T(8,128)(2,1)}, bf16[3,32,256]{2,1,0:T(8,128)(2,1)}, u32[]{:S(2)}, u32[]{:S(2)}) collective-permute-start(bf16[3,32,256]{2,1,0:T(8,128)(2,1)} %collective-permute-done.8), channel_id=1, source_target_pairs={{0,2},{2,0},{1,3},{3,1},{4,6},{6,4},{5,7},{7,5},{8,10},{10,8},{9,1... | collective-permute-start | bytes 147464 | tf_op jit(solution)/shard_map/ppermute | solution.py:15
  137.9 6.1 %collective-permute-start.10 = (bf16[3,32,256]{2,1,0:T(8,128)(2,1)}, bf16[3,32,256]{2,1,0:T(8,128)(2,1)}, u32[]{:S(2)}, u32[]{:S(2)}) collective-permute-start(bf16[3,32,256]{2,1,0:T(8,128)(2,1)} %collective-permute-done.9), channel_id=1, source_target_pairs={{0,4},{4,0},{1,5},{5,1},{2,6},{6,2},{3,7},{7,3},{8,12},{12,8},{9,1... | collective-permute-start | bytes 147464 | tf_op jit(solution)/shard_map/ppermute | solution.py:15
  144.0 65.4 %collective-permute-start.11 = (bf16[3,32,256]{2,1,0:T(8,128)(2,1)}, bf16[3,32,256]{2,1,0:T(8,128)(2,1)S(1)}, u32[]{:S(2)}, u32[]{:S(2)}) collective-permute-start(bf16[3,32,256]{2,1,0:T(8,128)(2,1)} %collective-permute-done.10), channel_id=1, source_target_pairs={{0,8},{8,0},{1,9},{9,1},{2,10},{10,2},{3,11},{11,3},{4,12},{12,4},... | collective-permute-start | bytes 147464 | tf_op jit(solution)/shard_map/ppermute | solution.py:15
  (100 other events, 601.3 us)
Sparse Core Ops, SparseCore 0:
  131.6 59.5 reduce-scatter.1
where the time goes:
time: 222 us; the launch traced here: 221 us
  other arithmetic  76.8 us (35%)
  blocking collectives  61.8 us (28%)
  local copies, waits for them, and re-layouts  21.1 us (10%)
  starting transfers between devices  19.4 us (9%)
  matrix products  18.8 us (8%)
  between operations  15.8 us (7%)
  waiting for transfers between devices  7.55 us (3%)
    psum x1, blocking collectives, local(): grad_kernel = lax.psum(local_kernel, 'lon')  61.8 us
    another operation x1, other arithmetic  22.2 us
    reduce_sum x3, other arithmetic, local(): jnp.sum(grad_conv * ext_wide[row_tap:row_tap + band_rows, col_tap:col_tap...  17.1 us
    reduce_sum x1, other arithmetic, local(): mean_z = jnp.mean(conv, axis=-1, keepdims=True)  15.9 us
    ppermute x8, starting transfers between devices, from_partner(): return lax.ppermute(block, axis, route)  10.4 us
    ppermute x2, starting transfers between devices, extended_2(): lax.ppermute(head, axis, [((i + 1) % count, i) for i in range(count)])  8.19 us
    dot_general x1, matrix products, local(): dhid = jnp.dot(dout, down_weight, preferred_element_type=jnp.float32)  6.25 us
    scatter-add x1, local copies, waits for them, and re-layouts, local(): grad_padded = grad_padded.at[:, :3].add(arrived[:, :3])  5.24 us
  transfers between devices with their start and end apart: 13, of which 5 were waited for; matrix products, arithmetic and copies ran while one was open for 13% of the time, Pallas kernels for 0%

commit v1 on v0

--- a/solution.py
+++ b/solution.py
@@ -107,7 +107,11 @@
                 )
             )
     local_kernel = jnp.stack(taps, axis=0).reshape(7, 7, channels) * factor
-    grad_kernel = lax.psum(local_kernel, "lon")
+    grad_kernel = local_kernel
+    for hop in (1, 2, 4, 8):
+        grad_kernel = grad_kernel + lax.ppermute(
+            grad_kernel, "lon", [(dev, dev ^ hop) for dev in range(16)]
+        )
     grad_pad = jnp.pad(grad_conv, ((6, 6), (6, 6), (0, 0)))
     grad_ext = jnp.zeros((band_rows + 6, band_cols + 6, channels), jnp.float32)
     for row_tap in range(7):

time: 222 us -> 185 us (0.83)
  blocking collectives: 61.8 us -> 0 us
  waiting for transfers between devices: 7.55 us -> 28.6 us
  starting transfers between devices: 19.4 us -> 22.9 us
  local copies, waits for them, and re-layouts: 21.1 us -> 24.1 us
  matrix products: 18.8 us -> 16.5 us
    psum x1 -> x0, blocking collectives: 61.8 us -> none  [local(): grad_kernel = lax.psum(local_kernel, 'lon')]
    reduce_scatter x1, waiting for transfers between devices: 0.01 us -> 9.81 us  [local(): lax.psum_scatter(jnp.concatenate([term_up, term_down], axis=1) * factor,...]
    ppermute x0 -> x4, waiting for transfers between devices: none -> 8.87 us  [local(): lax.ppermute(grad_kernel, 'lon', [(dev, dev ^ hop) for dev in range(16)])]
    another operation x1, local copies, waits for them, and re-layouts: 1.56 us -> 4.99 us  [local(): local_kernel = jnp.stack(taps, axis=0).reshape(7, 7, channels) * factor]
    ppermute x8, starting transfers between devices: 10.4 us -> 13.7 us  [from_partner(): return lax.ppermute(block, axis, route)]
    ppermute x8, waiting for transfers between devices: 4.87 us -> 7.23 us  [from_partner(): return lax.ppermute(block, axis, route)]
    dot_general x1, matrix products: 4.53 us -> 2.28 us  [local(): lax.dot_general(normed, dpre, contract_rows, preferred_element_type=jnp.f...]
  transfers between devices with their start and end apart: 13 -> 17, of which waited for: 5 -> 12; matrix products, arithmetic and copies ran while one was open for 13% -> 20% of each run, Pallas kernels for 0% -> 0%
where the time goes in v1:
time: 185 us
  other arithmetic  77.1 us (42%)
  waiting for transfers between devices  28.6 us (15%)
  local copies, waits for them, and re-layouts  24.1 us (13%)
  starting transfers between devices  22.9 us (12%)
  matrix products  16.5 us (9%)
  between operations  15.5 us (8%)
    another operation x1, other arithmetic  22.8 us
    reduce_sum x3, other arithmetic, local(): jnp.sum(grad_conv * ext_wide[row_tap:row_tap + band_rows, col_tap:col_tap...  17.8 us
    reduce_sum x1, other arithmetic, local(): mean_z = jnp.mean(conv, axis=-1, keepdims=True)  15.9 us
    ppermute x8, starting transfers between devices, from_partner(): return lax.ppermute(block, axis, route)  13.7 us
    reduce_scatter x1, waiting for transfers between devices, local(): lax.psum_scatter(jnp.concatenate([term_up, term_down], axis=1) * factor,...  9.81 us
    ppermute x4, waiting for transfers between devices, local(): lax.ppermute(grad_kernel, 'lon', [(dev, dev ^ hop) for dev in range(16)])  8.87 us
    ppermute x2, starting transfers between devices, extended_2(): lax.ppermute(head, axis, [((i + 1) % count, i) for i in range(count)])  8.19 us
    ppermute x8, waiting for transfers between devices, from_partner(): return lax.ppermute(block, axis, route)  7.23 us
  transfers between devices with their start and end apart: 17, of which 12 were waited for; matrix products, arithmetic and copies ran while one was open for 20% of the time, Pallas kernels for 0%

profile of v1, /device:TPU:0, one launch (start us, length us, event | category | flops | bytes accessed | tf_op | source)
XLA Modules:
  0.0 184.8 jit_solution(17779690968219646127)
XLA Ops:
  11.2 2.9 %collective-permute-start.1 = (bf16[3,32,256]{2,1,0:T(8,128)(2,1)S(1)}, bf16[3,32,256]{2,1,0:T(8,128)(2,1)S(1)}, u32[]{:S(2)}, u32[]{:S(2)}) collective-permute-start(bf16[3,32,256]{2,1,0:T(8,128)(2,1)S(1)} %collective-permute-done), channel_id=1, source_target_pairs={{0,2},{2,0},{1,3},{3,1},{4,6},{6,4},{5,7},{7,5},{8,10},{10,8},{9,1... | collective-permute-start | bytes 147464 | tf_op jit(solution)/shard_map/ppermute | solution.py:15
  20.3 3.0 %collective-permute-start.3 = (bf16[3,32,256]{2,1,0:T(8,128)(2,1)S(1)}, bf16[3,32,256]{2,1,0:T(8,128)(2,1)S(1)}, u32[]{:S(2)}, u32[]{:S(2)}) collective-permute-start(bf16[3,32,256]{2,1,0:T(8,128)(2,1)S(1)} %collective-permute-done.2), channel_id=1, source_target_pairs={{0,8},{8,0},{1,9},{9,1},{2,10},{10,2},{3,11},{11,3},{4,12},{12,4},... | collective-permute-start | bytes 147464 | tf_op jit(solution)/shard_map/ppermute | solution.py:15
  25.6 4.4 %collective-permute-start.5 = (bf16[70,3,256]{2,1,0:T(4,128)(2,1)S(1)}, bf16[70,3,256]{2,1,0:T(4,128)(2,1)S(1)}, u32[]{:S(2)}, u32[]{:S(2)}) collective-permute-start(bf16[70,3,256]{2,1,0:T(4,128)(2,1)S(1)} %get-tuple-element.97), channel_id=1, source_target_pairs={{1,0},{2,1},{3,2},{4,3},{5,4},{6,5},{7,6},{8,7},{9,8},{10,9},{11,1... | collective-permute-start | bytes 322568 | tf_op jit(solution)/shard_map/ppermute | solution.py:27
  30.3 2.7 %collective-permute-done.4 = bf16[70,3,256]{2,1,0:T(4,128)(2,1)S(1)} collective-permute-done((bf16[70,3,256]{2,1,0:T(4,128)(2,1)S(1)}, bf16[70,3,256]{2,1,0:T(4,128)(2,1)S(1)}, u32[]{:S(2)}, u32[]{:S(2)}) %collective-permute-start.4) | collective-permute-done | bytes 107552 | tf_op jit(solution)/shard_map/ppermute | solution.py:25
  35.2 15.9 %fusion.115 = (f32[64,32]{1,0:T(8,128)S(1)}, f32[64,32,256]{2,1,0:T(8,128)}) fusion(f32[70,38,256]{2,1,0:T(8,128)S(1)} %maximum_convert_fusion, f32[256]{0:T(256)S(1)} %bitcast.211, f32[256]{0:T(256)S(1)} %bitcast.213, f32[256]{0:T(256)S(1)} %bitcast.119, f32[256]{0:T(256)S(1)} %bitcast.121, f32[256]{0:T(256)S(1)} %bitcast.123, f32[256]{0:T(256)S(1)} %bitcast.125, ...), kind=kLoop, calls=%fused_computation.242 | loop fusion | flops 51378176 | bytes 104915968 | tf_op jit(solution)/shard_map/reduce_sum | solution.py:62
  51.1 2.4 %multiply_reduce_fusion.51 = f32[64,32]{1,0:T(8,128)S(1)} fusion(f32[64,32,256]{2,1,0:T(8,128)} %get-tuple-element.93, f32[64,32]{1,0:T(8,128)S(1)} %broadcast_multiply_fusion.3), kind=kLoop, calls=%fused_computation.216 | loop fusion | flops 1570816 | bytes 2113536 | tf_op jit(solution)/shard_map/reduce_sum | solution.py:64
  55.6 4.2 %fusion.7 = f32[256,1024]{1,0:T(8,128)} fusion(bf16[2048,256]{1,0:T(8,128)(2,1)S(1)} %bitcast.115, f32[2048,1024]{1,0:T(8,128)S(1)} %fusion.121), kind=kOutput, calls=%fused_computation.59 | convolution fusion | flops 1092616192 | bytes 10485760 | tf_op jit(solution)/shard_map/dot_general | solution.py:83
  59.7 6.3 %fusion.6 = bf16[2048,1024]{1,0:T(8,128)(2,1)S(1)} fusion(f32[2048,1024]{1,0:T(8,128)S(1)} %fusion.121, bf16[2048,256]{1,0:T(8,128)(2,1)S(1)} %bitcast.116, bf16[256,1024]{1,0:T(8,128)(2,1)S(1)} %copy-done.87), kind=kOutput, calls=%fused_computation.57 | convolution fusion | flops 1115684864 | bytes 14155776 | tf_op jit(solution)/shard_map/dot_general | solution.py:75
  66.0 2.3 %fusion.122 = f32[256,1024]{1,0:T(8,128)} fusion(bf16[2048,256]{1,0:T(8,128)(2,1)S(1)} %bitcast.114, bf16[2048,1024]{1,0:T(8,128)(2,1)S(1)} %fusion.6), kind=kOutput, calls=%fused_computation.249 | convolution fusion | flops 1073741824 | bytes 6291456 | tf_op jit(solution)/shard_map/dot_general | solution.py:82
  68.3 2.6 %multiply_reduce_fusion.50 = (f32[2048]{0:T(1024)S(1)}, f32[2048,256]{1,0:T(8,128)}) fusion(f32[256]{0:T(256)S(1)} %copy-done.13, bf16[2048,1024]{1,0:T(8,128)(2,1)S(1)} %fusion.6, bf16[256,1024]{1,0:T(8,128)(2,1)S(1)} %copy-done), kind=kOutput, calls=%fused_computation.214 | convolution fusion | flops 1074788352 | bytes 6824960 | tf_op jit(solution)/shard_map/dot_general | solution.py:92
  70.9 2.9 %multiply_reduce_fusion.49 = f32[64,32]{1,0:T(8,128)S(1)} fusion(f32[64,32,256]{2,1,0:T(8,128)} %bitcast.112, f32[64,32,256]{2,1,0:T(8,128)} %get-tuple-element.93, f32[256]{0:T(256)S(1)} %copy-done.13, f32[64,32]{1,0:T(8,128)S(1)} %add_rsqrt_fusion, f32[64,32]{1,0:T(8,128)S(1)} %broadcast_multiply_fusion.3), kind=kLoop, calls=%fused_computation.213 | loop fusion | flops 2619392 | bytes 4219904 | tf_op jit(solution)/shard_map/reduce_sum | solution.py:97
  74.4 6.7 %multiply_reduce_fusion = (f32[256]{0:T(256)}, f32[256]{0:T(256)}, f32[256]{0:T(256)}, f32[256]{0:T(256)}, f32[256]{0:T(256)}, /*index=5*/f32[256]{0:T(256)}, f3...) fusion(f32[70,38,256]{2,1,0:T(8,128)S(1)} %maximum_convert_fusi, ...), kind=kLoop, calls=%fused_computation.163 | loop fusion | flops 22539776 | bytes 44092416 | tf_op jit(solution)/shard_map/reduce_sum | solution.py:103
  81.4 4.5 %multiply_reduce_fusion.36 = (f32[256]{0:T(256)}, f32[256]{0:T(256)}, f32[256]{0:T(256)}, f32[256]{0:T(256)}, f32[256]{0:T(256)}, /*index=5*/f32[256]{0:T(256)},...) fusion(f32[64,32,256]{2,1,0:T(8,128)S(1)} %get-tuple-element.89, ...), kind=kLoop, calls=%fused_computation.199 | loop fusion | flops 13628160 | bytes 29373440 | tf_op jit(solution)/shard_map/reduce_sum | solution.py:103
  86.3 22.8 %fusion.113 = (bf16[70,38,256]{2,1,0:T(8,128)(2,1)}, f32[70,38,256]{2,1,0:T(8,128)}) fusion(f32[256]{0:T(256)S(1)} %bitcast.212, f32[256]{0:T(256)S(1)} %bitcast.214, f32[256]{0:T(256)S(1)} %bitcast.120, f32[256]{0:T(256)S(1)} %bitcast.122, f32[256]{0:T(256)S(1)} %bitcast.124, f32[256]{0:T(256)S(1)} %bitcast.126, f32[256]{0:T(256)S(1)} %bitcast.128, ...), kind=kLoop, calls=%fused_computation.241 | loop fusion | flops 66734080 | bytes 6233088 | tf_op jit(solution)/shard_map/convert.3
  113.2 3.8 %collective-permute-start.7 = (bf16[70,3,256]{2,1,0:T(4,128)(2,1)}, bf16[70,3,256]{2,1,0:T(4,128)(2,1)}, u32[]{:S(2)}, u32[]{:S(2)}) collective-permute-start(bf16[70,3,256]{2,1,0:T(4,128)(2,1)} %get-tuple-element.95), channel_id=1, source_target_pairs={{1,0},{2,1},{3,2},{4,3},{5,4},{6,5},{7,6},{8,7},{9,8},{10,9},{11,1... | collective-permute-start | bytes 322568 | tf_op jit(solution)/shard_map/ppermute | solution.py:27
  117.0 6.6 %multiply_reduce_fusion.18 = (f32[256]{0:T(256)S(1)}, f32[256]{0:T(256)S(1)}, f32[256]{0:T(256)S(1)}, f32[256]{0:T(256)S(1)}, f32[256]{0:T(256)S(1)}, /*index=5*...) fusion(f32[64,32,256]{2,1,0:T(8,128)} %copy-done.3, ...), kind=kLoop, calls=%fused_computation.181 | loop fusion | flops 18869760 | bytes 39864320 | tf_op jit(solution)/shard_map/reduce_sum | solution.py:103
  123.6 5.0 %stack.199 = f32[49,256]{1,0:T(8,128)S(1)} concatenate(f32[1,256]{1,0:T(1,128)} %bitcast.263, f32[1,256]{1,0:T(1,128)} %bitcast.262, f32[1,256]{1,0:T(1,128)} %bitcast.261, f32[1,256]{1,0:T(1,128)} %bitcast.260, f32[1,256]{1,0:T(1,128)} %bitcast.259, f32[1,256]{1,0:T(1,128)} %bitcast.258, f32[1,256]{1,0:T(1,128)} %bitcast.257, f32[1,256]{1,0:T(1,128)} %bitcast.256, ...), dimensions={0} | concatenate | bytes 100352 | tf_op jit(solution)/shard_map/stack | solution.py:109
  128.7 2.3 %slice.866 = f32[70,32,256]{2,1,0:T(8,128)S(1)} slice(f32[70,38,256]{2,1,0:T(8,128)} %get-tuple-element.91), slice={[0:70], [3:35], [0:256]} | slice | bytes 4587520 | tf_op jit(solution)/shard_map/slice | solution.py:128
  132.5 5.9 %scatter-add.10 = f32[70,32,256]{2,1,0:T(8,128)S(1)} dynamic-update-slice(f32[70,32,256]{2,1,0:T(8,128)S(1)} %slice.866, f32[70,3,256]{2,1,0:T(4,128)S(1)} %convert_add_fusion.1, s32[]{:T(128)} %constant.108.clone.1, s32[]{:T(128)} %constant.108.clone.1, s32[]{:T(128)} %constant.108.clone.1) | dynamic-update-slice | bytes 430084 | tf_op jit(solution)/shard_map/scatter-add | solution.py:129
  139.7 4.1 %scatter-add.11 = f32[70,32,256]{2,1,0:T(8,128)S(1)} dynamic-update-slice(f32[70,32,256]{2,1,0:T(8,128)S(1)} %scatter-add.10, f32[70,3,256]{2,1,0:T(4,128)S(1)} %slice_add_fusion, s32[]{:T(128)} %constant.108.clone.1, s32[]{:T(128)} %constant.109.clone.1, s32[]{:T(128)} %constant.108.clone.1) | dynamic-update-slice | bytes 430084 | tf_op jit(solution)/shard_map/scatter-add | solution.py:130
  146.5 2.7 %collective-permute-done.13 = f32[7,7,256]{2,1,0:T(8,128)S(1)} collective-permute-done((f32[7,7,256]{2,1,0:T(8,128)S(1)}, f32[7,7,256]{2,1,0:T(8,128)S(1)}, u32[]{:S(2)}, u32[]{:S(2)}) %collective-permute-start.13) | collective-permute-done | bytes 50208 | tf_op jit(solution)/shard_map/ppermute | solution.py:112
  151.3 5.1 %collective-permute-done.14 = f32[7,7,256]{2,1,0:T(8,128)S(1)} collective-permute-done((f32[7,7,256]{2,1,0:T(8,128)S(1)}, f32[7,7,256]{2,1,0:T(8,128)S(1)}, u32[]{:S(2)}, u32[]{:S(2)}) %collective-permute-start.14) | collective-permute-done | bytes 50208 | tf_op jit(solution)/shard_map/ppermute | solution.py:112
  163.4 3.2 %fusion.107 = bf16[64,32,256]{2,1,0:T(8,128)(2,1)} fusion(bf16[64,32,256]{2,1,0:T(8,128)(2,1)} %param.16, f32[64,32,256]{2,1,0:T(8,128)} %fusion.108, f32[64,32]{1,0:T(8,128)S(1)} %copy-done.11), kind=kLoop, calls=%fused_computation.161 | loop fusion | flops 2097152 | bytes 4202496 | tf_op jit(solution)/shard_map/convert_element_type | solution.py:141
  166.6 9.8 %reduce-scatter.2.cloned.1.call-done = f32[16,2048]{1,0:T(8,128)} async-done(((f32[256,2048]{1,0:T(8,128)}), f32[16,2048]{1,0:T(8,128)}) %reduce-scatter.2.cloned.1.call-update) | async-done | bytes 131088 | tf_op jit(solution)/shard_map/reduce_scatter | solution.py:84
  (238 shorter events, 37.3 us)
Async XLA Ops:
  7.2 47.1 %copy-start = (bf16[256,1024]{1,0:T(8,128)(2,1)S(1)}, bf16[256,1024]{1,0:T(8,128)(2,1)}, u32[]{:S(2)}) copy-start(bf16[256,1024]{1,0:T(8,128)(2,1)} %param.19) | copy-start | bytes 1572868
  7.2 169.2 %reduce-scatter.2.cloned.1.call-start = ((), (), s32[]{:S(2)}) async-start(), calls=%async_computation.1 | async-start | bytes 2228224 | tf_op jit(solution)/shard_map/reduce_scatter | solution.py:84
  9.8 23.2 %copy-start.4 = (bf16[64,32,256]{2,1,0:T(8,128)(2,1)}, bf16[64,32,256]{2,1,0:T(8,128)(2,1)S(1)}, u32[]{:S(2)}) copy-start(bf16[64,32,256]{2,1,0:T(8,128)(2,1)S(1)} %broadcast_multiply_fusion) | copy-start | bytes 3145732
  9.8 1.4 collective-permute-start
  10.4 22.6 %copy-start.10 = (f32[64,32]{1,0:T(8,128)}, f32[64,32]{1,0:T(8,128)S(1)}, u32[]{:S(2)}) copy-start(f32[64,32]{1,0:T(8,128)S(1)} %copy.14) | copy-start | bytes 24580
  11.2 4.9 %collective-permute-start.1 = (bf16[3,32,256]{2,1,0:T(8,128)(2,1)S(1)}, bf16[3,32,256]{2,1,0:T(8,128)(2,1)S(1)}, u32[]{:S(2)}, u32[]{:S(2)}) collective-permute-start(bf16[3,32,256]{2,1,0:T(8,128)(2,1)S(1)} %collective-permute-done), channel_id=1, source_target_pairs={{0,2},{2,0},{1,3},{3,1},{4,6},{6,4},{5,7},{7,5},{8,10},{10,8},{9,1... | collective-permute-start | bytes 147464 | tf_op jit(solution)/shard_map/ppermute | solution.py:15
  16.1 4.1 %collective-permute-start.2 = (bf16[3,32,256]{2,1,0:T(8,128)(2,1)S(1)}, bf16[3,32,256]{2,1,0:T(8,128)(2,1)S(1)}, u32[]{:S(2)}, u32[]{:S(2)}) collective-permute-start(bf16[3,32,256]{2,1,0:T(8,128)(2,1)S(1)} %collective-permute-done.1), channel_id=1, source_target_pairs={{0,4},{4,0},{1,5},{5,1},{2,6},{6,2},{3,7},{7,3},{8,12},{12,8},{9,1... | collective-permute-start | bytes 147464 | tf_op jit(solution)/shard_map/ppermute | solution.py:15
  18.2 16.6 %copy-start.14 = (f32[1,1,256]{2,1,0:T(1,128)}, f32[1,1,256]{2,1,0:T(1,128)S(1)}, u32[]{:S(2)}) copy-start(f32[1,1,256]{2,1,0:T(1,128)S(1)} %get-tuple-element.113) | copy-start | bytes 3076
  18.2 16.6 %copy-start.16 = (f32[1,1,256]{2,1,0:T(1,128)}, f32[1,1,256]{2,1,0:T(1,128)S(1)}, u32[]{:S(2)}) copy-start(f32[1,1,256]{2,1,0:T(1,128)S(1)} %get-tuple-element.114) | copy-start | bytes 3076
  20.3 5.1 %collective-permute-start.3 = (bf16[3,32,256]{2,1,0:T(8,128)(2,1)S(1)}, bf16[3,32,256]{2,1,0:T(8,128)(2,1)S(1)}, u32[]{:S(2)}, u32[]{:S(2)}) collective-permute-start(bf16[3,32,256]{2,1,0:T(8,128)(2,1)S(1)} %collective-permute-done.2), channel_id=1, source_target_pairs={{0,8},{8,0},{1,9},{9,1},{2,10},{10,2},{3,11},{11,3},{4,12},{12,4},... | collective-permute-start | bytes 147464 | tf_op jit(solution)/shard_map/ppermute | solution.py:15
  25.6 7.4 %collective-permute-start.4 = (bf16[70,3,256]{2,1,0:T(4,128)(2,1)S(1)}, bf16[70,3,256]{2,1,0:T(4,128)(2,1)S(1)}, u32[]{:S(2)}, u32[]{:S(2)}) collective-permute-start(bf16[70,3,256]{2,1,0:T(4,128)(2,1)S(1)} %get-tuple-element.96), channel_id=1, source_target_pairs={{0,1},{1,2},{2,3},{3,4},{4,5},{5,6},{6,7},{7,8},{8,9},{9,10},{10,1... | collective-permute-start | bytes 322568 | tf_op jit(solution)/shard_map/ppermute | solution.py:25
  25.6 7.3 %collective-permute-start.5 = (bf16[70,3,256]{2,1,0:T(4,128)(2,1)S(1)}, bf16[70,3,256]{2,1,0:T(4,128)(2,1)S(1)}, u32[]{:S(2)}, u32[]{:S(2)}) collective-permute-start(bf16[70,3,256]{2,1,0:T(4,128)(2,1)S(1)} %get-tuple-element.97), channel_id=1, source_target_pairs={{1,0},{2,1},{3,2},{4,3},{5,4},{6,5},{7,6},{8,7},{9,8},{10,9},{11,1... | collective-permute-start | bytes 322568 | tf_op jit(solution)/shard_map/ppermute | solution.py:27
  86.3 22.9 %copy-start.8 = (f32[256,1024]{1,0:T(8,128)S(1)}, f32[256,1024]{1,0:T(8,128)}, u32[]{:S(2)}) copy-start(f32[256,1024]{1,0:T(8,128)} %fusion.7) | copy-start | bytes 3145732
  86.3 22.9 %copy-start.9 = (f32[256,1024]{1,0:T(8,128)S(1)}, f32[256,1024]{1,0:T(8,128)}, u32[]{:S(2)}) copy-start(f32[256,1024]{1,0:T(8,128)} %fusion.122) | copy-start | bytes 3145732
  112.6 18.4 %collective-permute-start.6 = (bf16[70,3,256]{2,1,0:T(4,128)(2,1)S(1)}, bf16[70,3,256]{2,1,0:T(4,128)(2,1)}, u32[]{:S(2)}, u32[]{:S(2)}) collective-permute-start(bf16[70,3,256]{2,1,0:T(4,128)(2,1)S(1)} %get-tuple-element.94), channel_id=1, source_target_pairs={{0,1},{1,2},{2,3},{3,4},{4,5},{5,6},{6,7},{7,8},{8,9},{9,10},{10,1... | collective-permute-start | bytes 322568 | tf_op jit(solution)/shard_map/ppermute | solution.py:25
  113.2 17.8 %collective-permute-start.7 = (bf16[70,3,256]{2,1,0:T(4,128)(2,1)}, bf16[70,3,256]{2,1,0:T(4,128)(2,1)}, u32[]{:S(2)}, u32[]{:S(2)}) collective-permute-start(bf16[70,3,256]{2,1,0:T(4,128)(2,1)} %get-tuple-element.95), channel_id=1, source_target_pairs={{1,0},{2,1},{3,2},{4,3},{5,4},{6,5},{7,6},{8,7},{9,8},{10,9},{11,1... | collective-permute-start | bytes 322568 | tf_op jit(solution)/shard_map/ppermute | solution.py:27
  128.6 15.7 %collective-permute-start.12 = (f32[7,7,256]{2,1,0:T(8,128)S(1)}, f32[7,7,256]{2,1,0:T(8,128)S(1)}, u32[]{:S(2)}, u32[]{:S(2)}) collective-permute-start(f32[7,7,256]{2,1,0:T(8,128)S(1)} %mul.1497), channel_id=1, source_target_pairs={{0,1},{1,0},{2,3},{3,2},{4,5},{5,4},{6,7},{7,6},{8,9},{9,8},{10,11... | collective-permute-start | bytes 150536 | tf_op jit(solution)/shard_map/ppermute | solution.py:112
  143.8 1.4 collective-permute-start.8
  144.4 4.8 %collective-permute-start.13 = (f32[7,7,256]{2,1,0:T(8,128)S(1)}, f32[7,7,256]{2,1,0:T(8,128)S(1)}, u32[]{:S(2)}, u32[]{:S(2)}) collective-permute-start(f32[7,7,256]{2,1,0:T(8,128)S(1)} %add.452), channel_id=1, source_target_pairs={{0,2},{1,3},{2,0},{3,1},{4,6},{5,7},{6,4},{7,5},{8,10},{9,11},{10,... | collective-permute-start | bytes 150536 | tf_op jit(solution)/shard_map/ppermute | solution.py:112
  145.3 4.6 %collective-permute-start.9 = (bf16[3,32,256]{2,1,0:T(8,128)(2,1)S(1)}, bf16[3,32,256]{2,1,0:T(8,128)(2,1)S(1)}, u32[]{:S(2)}, u32[]{:S(2)}) collective-permute-start(bf16[3,32,256]{2,1,0:T(8,128)(2,1)S(1)} %collective-permute-done.8), channel_id=1, source_target_pairs={{0,2},{2,0},{1,3},{3,1},{4,6},{6,4},{5,7},{7,5},{8,10},{10,8},{9,1... | collective-permute-start | bytes 147464 | tf_op jit(solution)/shard_map/ppermute | solution.py:15
  149.2 7.2 %collective-permute-start.14 = (f32[7,7,256]{2,1,0:T(8,128)S(1)}, f32[7,7,256]{2,1,0:T(8,128)S(1)}, u32[]{:S(2)}, u32[]{:S(2)}) collective-permute-start(f32[7,7,256]{2,1,0:T(8,128)S(1)} %add.453), channel_id=1, source_target_pairs={{0,4},{1,5},{2,6},{3,7},{4,0},{5,1},{6,2},{7,3},{8,12},{9,13},{10,... | collective-permute-start | bytes 150536 | tf_op jit(solution)/shard_map/ppermute | solution.py:112
  149.9 7.7 %collective-permute-start.10 = (bf16[3,32,256]{2,1,0:T(8,128)(2,1)S(1)}, bf16[3,32,256]{2,1,0:T(8,128)(2,1)S(1)}, u32[]{:S(2)}, u32[]{:S(2)}) collective-permute-start(bf16[3,32,256]{2,1,0:T(8,128)(2,1)S(1)} %collective-permute-done.9), channel_id=1, source_target_pairs={{0,4},{4,0},{1,5},{5,1},{2,6},{6,2},{3,7},{7,3},{8,12},{12,8},{9,1... | collective-permute-start | bytes 147464 | tf_op jit(solution)/shard_map/ppermute | solution.py:15
  156.4 5.5 %collective-permute-start.15 = (f32[7,7,256]{2,1,0:T(8,128)S(1)}, f32[7,7,256]{2,1,0:T(8,128)S(1)}, u32[]{:S(2)}, u32[]{:S(2)}) collective-permute-start(f32[7,7,256]{2,1,0:T(8,128)S(1)} %add.454), channel_id=1, source_target_pairs={{0,8},{1,9},{2,10},{3,11},{4,12},{5,13},{6,14},{7,15},{8,0},{9,1},... | collective-permute-start | bytes 150536 | tf_op jit(solution)/shard_map/ppermute | solution.py:112
  157.5 5.1 %collective-permute-start.11 = (bf16[3,32,256]{2,1,0:T(8,128)(2,1)S(1)}, bf16[3,32,256]{2,1,0:T(8,128)(2,1)S(1)}, u32[]{:S(2)}, u32[]{:S(2)}) collective-permute-start(bf16[3,32,256]{2,1,0:T(8,128)(2,1)S(1)} %collective-permute-done.10), channel_id=1, source_target_pairs={{0,8},{8,0},{1,9},{9,1},{2,10},{10,2},{3,11},{11,3},{4,12},{12,4},... | collective-permute-start | bytes 147464 | tf_op jit(solution)/shard_map/ppermute | solution.py:15
  (81 other events, 496.2 us)
Sparse Core Ops, SparseCore 0:
  110.9 65.4 reduce-scatter.1
